TPU v7x, 512 devices: a whole 4x4x16 slice. The times are simulated.
512 devices in a mesh: grp: 16 (over y, x), tp: 32 (over z, core).
Axes of the slice: x: 4, y: 4, z: 16, core: 2. Of those that a mesh axis runs over, the one named last changes fastest.
Arguments:
- tokens: bfloat16 [6144, 5120], P('grp'), may hold values from -36 to 36
- trainer_panels: bfloat16 [64, 5120, 128], P('tp', 'grp'), may hold values from -0.078125 to 0.078125
- panel_home: int32 [48], replicated, may hold values from 0 to 63, as said below
- lengths: int32 [16, 4], P('grp'), may hold values from 1 to 192, 384 in all within a row
Outputs:
- context: float32 [6144, 4096], P(('grp', 'tp'))
Inputs may be any that keep to these rules, and one draw needn't show every extreme that they name: `panel_home`: entries are distinct; entry p is 2 times the tp index of the trainer device that holds panel p, plus the panel's slot on that device. Panels 0 to 31 are query heads, the next 8 key heads, the last 8 value heads. Some trainer device holds 2 panels.
All inputs are finite; a program needn't handle non-finite values.
Results may differ from a plain program's by a relative error of at most 0.012.
Values may be sent and summed in bfloat16 or wider, within the bound.
A program may use at most 64 MiB of HBM per device.

v0:
```python
import jax
import jax.numpy as jnp
from jax import lax
from jax.sharding import PartitionSpec as P


def on_device(tokens, trainer_panels, panel_home, lengths):
    tp_count = lax.axis_size("tp")
    member_id = lax.axis_index("tp")
    kv_count = (panel_home.shape[0] - tp_count) // 2
    group_size = tp_count // kv_count
    slot_count = trainer_panels.shape[0]
    head_dim = trainer_panels.shape[2]
    needed = jnp.stack(
        [
            member_id,
            tp_count + member_id // group_size,
            tp_count + kv_count + member_id // group_size,
        ]
    )
    wanted = panel_home[needed]
    peer_ids = jnp.arange(tp_count, dtype=jnp.int32)
    reader_need = jnp.stack(
        [peer_ids, tp_count + peer_ids // group_size, tp_count + kv_count + peer_ids // group_size],
        axis=1,
    )
    reader_home = panel_home[reader_need]
    local_slot = reader_home - member_id * slot_count
    owned_here = (local_slot >= 0) & (local_slot < slot_count)
    picked = trainer_panels[jnp.clip(local_slot, 0, slot_count - 1)]
    outbound = jnp.where(owned_here[:, :, None, None], picked, jnp.zeros_like(picked))
    arrived = lax.all_to_all(outbound, "tp", split_axis=0, concat_axis=0, tiled=True)
    source = wanted // slot_count
    selected = jnp.stack([arrived[source[need_pos], need_pos] for need_pos in range(3)], axis=1)
    full_panels = lax.all_gather(selected, "grp", axis=0, tiled=True)
    weights = full_panels.reshape(full_panels.shape[0], 3 * head_dim)
    projected = jnp.dot(tokens, weights, preferred_element_type=jnp.float32).astype(jnp.bfloat16)
    query_rows = projected[:, :head_dim]
    key_rows = projected[:, head_dim : 2 * head_dim]
    value_rows = projected[:, 2 * head_dim :]
    seq_total = query_rows.shape[0]
    position = jnp.arange(seq_total, dtype=jnp.int32)
    bounds = jnp.cumsum(lengths[0])
    segment = jnp.sum((position[:, None] >= bounds[None, :]).astype(jnp.int32), axis=1)
    allowed = (segment[:, None] == segment[None, :]) & (position[None, :] <= position[:, None])
    score_scale = head_dim ** (-0.5)
    scores = (
        lax.dot_general(
            query_rows, key_rows, (((1,), (1,)), ((), ())), preferred_element_type=jnp.float32
        )
        * score_scale
    )
    masked = jnp.where(allowed, scores, -jnp.inf)
    row_peak = jnp.max(masked, axis=1, keepdims=True)
    row_exp = jnp.exp(masked - row_peak)
    attn_probs = (row_exp / jnp.sum(row_exp, axis=1, keepdims=True)).astype(jnp.bfloat16)
    context = jnp.dot(attn_probs, value_rows, preferred_element_type=jnp.float32)
    return lax.all_to_all(context, "tp", split_axis=0, concat_axis=1, tiled=True)


def solution(mesh):
    placed = (P("grp", None), P("tp", "grp", None), P(), P("grp", None))
    return jax.shard_map(
        on_device, mesh=mesh, in_specs=placed, out_specs=P(("grp", "tp"), None), check_vma=False
    )
```

profile of v0, /device:TPU:1, one launch (start us, length us, event | category | flops | bytes accessed | tf_op | source)
XLA Modules:
  0.0 502.2 jit_solution(18027963017694480111)
XLA Ops:
  6.5 0.0 copy-start
  6.5 0.0 copy-start.1
  6.6 0.1 copy.31
  6.7 0.1 reshape.305
  6.8 0.4 copy-done.1
  7.2 1.2 gather_fusion
  8.5 0.1 min.12
  8.6 0.1 copy.32
  8.7 0.1 copy.35
  8.8 0.1 reshape.313
  8.9 0.1 reshape.339
  9.0 0.0 copy-done
  9.0 6.4 %gather_fusion.1 = bf16[96,320,128]{2,1,0:T(8,128)(2,1)} fusion(bf16[2,320,128]{2,1,0:T(8,128)(2,1)S(1)} %copy-done, s32[1024]{0:T(1024)S(1)} %pad_clamp_fusion.1), kind=kCustom, calls=%fused_computation.1 | custom fusion | bytes 15729024 | tf_op jit(solution)/shard_map/gather | solution.py:30
  15.4 6.9 %broadcast_select_fusion = bf16[32,3,320,128]{3,2,1,0:T(8,128)(2,1)} fusion(bf16[32,3,320,128]{3,2,1,0:T(8,128)(2,1)} %bitcast.34, pred[32,3]{1,0:T(8,128)(4,1)S(1)} %reshape.339), kind=kLoop, calls=%fused_computation.3 | loop fusion | flops 3932160 | bytes 15728736 | tf_op jit(solution)/shard_map/jit(_where)/select_n | solution.py:31
  22.3 0.0 copy-start.2
  22.3 17.1 %all-to-all-start = ((bf16[32,3,320,128]{3,2,1,0:T(8,128)(2,1)}), bf16[32,3,320,128]{3,2,1,0:T(8,128)(2,1)}, u32[]{:S(2)}, u32[]{:S(2)}) async-start(bf16[32,3,320,128]{3,2,1,0:T(8,128)(2,1)} %broadcast_select_fusion), calls=%async_computation | async-start | bytes 15728640 | tf_op jit(solution)/shard_map/all_to_all | solution.py:32
  39.4 0.0 all-gather.2.cloned.1.call-start
  39.5 0.1 fusion.8
  39.6 0.6 gather_fusion.2
  40.2 0.7 fusion.9
  46.5 332.2 %all-to-all-done = bf16[32,3,320,128]{3,2,1,0:T(8,128)(2,1)} async-done(((bf16[32,3,320,128]{3,2,1,0:T(8,128)(2,1)}), bf16[32,3,320,128]{3,2,1,0:T(8,128)(2,1)}, u32[]{:S(2)}, u32[]{:S(2)}) %all-to-all-start) | async-done | bytes 7864352 | tf_op jit(solution)/shard_map/all_to_all | solution.py:32
  378.6 1.0 dynamic-slice_bitcast_fusion.2
  379.6 0.7 pad_maximum_fusion
  380.3 0.0 all-gather.2.cloned.1.call-update
  380.4 0.0 copy-done.2
  380.4 0.2 reduce-window.8
  380.6 0.1 convert_reduce_fusion
  380.7 66.1 %all-gather.2.cloned.1.call-done = bf16[5120,3,128]{2,0,1:T(8,128)(2,1)} async-done(((bf16[320,3,128]{2,0,1:T(8,128)(2,1)}), bf16[5120,3,128]{2,0,1:T(8,128)(2,1)}) %all-gather.2.cloned.1.call-update) | async-done | bytes 3932176 | tf_op jit(solution)/shard_map/all_gather | solution.py:35
  446.8 6.3 %copy.36 = bf16[5120,3,128]{0,2,1:T(8,128)(2,1)} copy(bf16[5120,3,128]{2,0,1:T(8,128)(2,1)} %all-gather.2.cloned.1.call-done) | data formatting | bytes 7864320 | tf_op jit(solution)/shard_map/all_gather | solution.py:35
  453.1 5.5 %fusion.1 = bf16[384,384]{0,1:T(8,128)(2,1)S(1)} fusion(bf16[5120,384]{0,1:T(8,128)(2,1)} %bitcast.35, bf16[384,5120]{1,0:T(8,128)(2,1)} %param.4), kind=kOutput, calls=%fused_computation.7 | convolution fusion | flops 1510096896 | bytes 8159232 | tf_op jit(solution)/shard_map/dot_general | solution.py:37
  458.6 0.3 fusion.10
  458.9 0.1 fusion.3
  459.1 0.3 fusion.4
  459.4 35.0 %all_to_all.24 = f32[32,12,128]{2,1,0:T(8,128)S(1)} all-to-all(f32[32,12,128]{2,1,0:T(8,128)S(1)} %all_to_all.18), channel_id=1, replica_groups=mesh['grp'=16,'tp'=32] {'tp'}, dimensions={0} | all-to-all | bytes 393216 | tf_op jit(solution)/shard_map/all_to_all | solution.py:58
  494.4 0.1 copy.37
  494.5 0.9 copy.38
  (12 shorter events, 0.1 us)
Async XLA Ops:
  6.5 2.5 copy-start
  6.5 0.7 copy-start.1
  22.3 358.1 %copy-start.2 = (s32[1,4]{1,0:T(1,128)S(1)}, s32[1,4]{1,0:T(1,128)}, u32[]{:S(2)}) copy-start(s32[1,4]{1,0:T(1,128)} %param.7) | copy-start | bytes 52
  22.3 356.3 %all-to-all-start = ((bf16[32,3,320,128]{3,2,1,0:T(8,128)(2,1)}), bf16[32,3,320,128]{3,2,1,0:T(8,128)(2,1)}, u32[]{:S(2)}, u32[]{:S(2)}) async-start(bf16[32,3,320,128]{3,2,1,0:T(8,128)(2,1)} %broadcast_select_fusion), calls=%async_computation | async-start | bytes 15728640 | tf_op jit(solution)/shard_map/all_to_all | solution.py:32
  39.4 407.3 %all-gather.2.cloned.1.call-start = ((), (), s32[]{:S(2)}) async-start(), calls=%async_computation.2 | async-start | bytes 4177920 | tf_op jit(solution)/shard_map/all_gather | solution.py:35
Sparse Core Ops, SparseCore 0:
  380.5 66.2 all-gather.1
where the time goes:
time: 503 us; the launch traced here: 502 us
  waiting for transfers between devices  398 us (79%)
  blocking collectives  35 us (7%)
  between operations  19.1 us (4%)
  local copies, waits for them, and re-layouts  18.3 us (4%)
  starting transfers between devices  17.2 us (3%)
  other arithmetic  8.16 us (2%)
  matrix products  6.13 us (1%)
    all_to_all x1, waiting for transfers between devices, on_device(): lax.all_to_all(outbound, 'tp', split_axis=0, concat_axis=0, tiled=True)  332 us
    all_gather x1, waiting for transfers between devices, on_device(): full_panels = lax.all_gather(selected, 'grp', axis=0, tiled=True)  66.1 us
    all_to_all x1, blocking collectives, on_device(): lax.all_to_all(context, 'tp', split_axis=0, concat_axis=1, tiled=True)  35 us
    all_to_all x1, starting transfers between devices, on_device(): lax.all_to_all(outbound, 'tp', split_axis=0, concat_axis=0, tiled=True)  17.1 us
  transfers between devices with their start and end apart: 2, of which 2 were waited for; matrix products, arithmetic and copies ran while one was open for 0% of the time, Pallas kernels for 0%

commit v1 on v0

--- a/solution.py
+++ b/solution.py
@@ -32,7 +32,26 @@
     arrived = lax.all_to_all(outbound, "tp", split_axis=0, concat_axis=0, tiled=True)
     source = wanted // slot_count
     selected = jnp.stack([arrived[source[need_pos], need_pos] for need_pos in range(3)], axis=1)
-    full_panels = lax.all_gather(selected, "grp", axis=0, tiled=True)
+    count, index, rows = (lax.axis_size("grp"), lax.axis_index("grp"), selected.shape[0])
+    ahead = [(i, (i + 1) % count) for i in range(count)]
+    backward = [(i, (i - 1) % count) for i in range(count)]
+    result = jnp.zeros(
+        (*selected.shape[:0], count * rows, *selected.shape[0 + 1 :]), selected.dtype
+    )
+    result = lax.dynamic_update_slice_in_dim(result, selected, index * rows, axis=0)
+    from_left = from_right = selected
+    halfway = count // 2
+    for step in range(1, halfway + 1):
+        from_left = lax.ppermute(from_left, "grp", ahead)
+        result = lax.dynamic_update_slice_in_dim(
+            result, from_left, (index - step) % count * rows, axis=0
+        )
+        if step < count - halfway:
+            from_right = lax.ppermute(from_right, "grp", backward)
+            result = lax.dynamic_update_slice_in_dim(
+                result, from_right, (index + step) % count * rows, axis=0
+            )
+    full_panels = result
     weights = full_panels.reshape(full_panels.shape[0], 3 * head_dim)
     projected = jnp.dot(tokens, weights, preferred_element_type=jnp.float32).astype(jnp.bfloat16)
     query_rows = projected[:, :head_dim]

time: 503 us -> 570 us (1.13)
  starting transfers between devices: 17.2 us -> 79.6 us
  local copies, waits for them, and re-layouts: 18.3 us -> 73.8 us
  waiting for transfers between devices: 398 us -> 352 us
  between operations: 19.1 us -> 6.31 us
  blocking collectives: 35 us -> 42.4 us
    all_gather x1 -> x0, waiting for transfers between devices: 66.1 us -> none  [on_device(): full_panels = lax.all_gather(selected, 'grp', axis=0, tiled=True)]
    ppermute x0 -> x15, starting transfers between devices: none -> 62.5 us  [the longest x7 45.8 us: on_device(): from_right = lax.ppermute(from_right, 'grp', backward)]
    dynamic_update_slice x0 -> x16, local copies, waits for them, and re-layouts: none -> 59.1 us  [the longest x8 29.2 us: on_device(): lax.dynamic_update_slice_in_dim(result, from_left, (index - step) % count...]
    ppermute x0 -> x15, waiting for transfers between devices: none -> 20.3 us  [the longest x8 20.3 us: on_device(): from_left = lax.ppermute(from_left, 'grp', ahead)]
    all_to_all x1, blocking collectives: 35 us -> 42.4 us  [on_device(): lax.all_to_all(context, 'tp', split_axis=0, concat_axis=1, tiled=True)]
    all_gather x1 -> x0, local copies, waits for them, and re-layouts: 6.33 us -> none  [on_device(): full_panels = lax.all_gather(selected, 'grp', axis=0, tiled=True)]
  transfers between devices with their start and end apart: 2 -> 16, of which waited for: 2 -> 8; matrix products, arithmetic and copies ran while one was open for 0% -> 10% of each run, Pallas kernels for 0% -> 0%
where the time goes in v1:
time: 570 us; the launch traced here: 568 us
  waiting for transfers between devices  352 us (62%)
  starting transfers between devices  79.6 us (14%)
  local copies, waits for them, and re-layouts  73.8 us (13%)
  blocking collectives  42.4 us (7%)
  other arithmetic  7.49 us (1%)
  between operations  6.31 us (1%)
  matrix products  6.13 us (1%)
    all_to_all x1, waiting for transfers between devices, on_device(): lax.all_to_all(outbound, 'tp', split_axis=0, concat_axis=0, tiled=True)  332 us
    ppermute x7, starting transfers between devices, on_device(): from_right = lax.ppermute(from_right, 'grp', backward)  45.8 us
    all_to_all x1, blocking collectives, on_device(): lax.all_to_all(context, 'tp', split_axis=0, concat_axis=1, tiled=True)  42.4 us
    dynamic_update_slice x8, local copies, waits for them, and re-layouts, on_device(): lax.dynamic_update_slice_in_dim(result, from_left, (index - step) % count...  29.2 us
    dynamic_update_slice x7, local copies, waits for them, and re-layouts, on_device(): lax.dynamic_update_slice_in_dim(result, from_right, (index + step) % coun...  26.5 us
    ppermute x8, waiting for transfers between devices, on_device(): from_left = lax.ppermute(from_left, 'grp', ahead)  20.3 us
    all_to_all x1, starting transfers between devices, on_device(): lax.all_to_all(outbound, 'tp', split_axis=0, concat_axis=0, tiled=True)  17.1 us
    ppermute x8, starting transfers between devices, on_device(): from_left = lax.ppermute(from_left, 'grp', ahead)  16.7 us
  transfers between devices with their start and end apart: 16, of which 8 were waited for; matrix products, arithmetic and copies ran while one was open for 10% of the time, Pallas kernels for 0%

profile of v1, /device:TPU:1, one launch (start us, length us, event | category | flops | bytes accessed | tf_op | source)
XLA Modules:
  0.0 568.2 jit_solution(1132833725522814117)
XLA Ops:
  0.0 0.1 copy.33
  0.1 0.1 reshape.305
  0.3 0.4 copy-done.1
  0.7 1.2 gather_fusion
  2.0 0.1 min.12
  2.1 0.1 copy.37
  2.2 0.1 reshape.313
  2.4 0.1 reshape.339
  2.5 6.4 %gather_fusion.1 = bf16[96,320,128]{2,1,0:T(8,128)(2,1)} fusion(bf16[2,320,128]{2,1,0:T(8,128)(2,1)S(1)} %copy-done, s32[1024]{0:T(1024)S(1)} %pad_clamp_fusion.1), kind=kCustom, calls=%fused_computation.1 | custom fusion | bytes 15729024 | tf_op jit(solution)/shard_map/gather | solution.py:30
  8.9 6.9 %broadcast_select_fusion = bf16[32,3,320,128]{3,2,1,0:T(8,128)(2,1)} fusion(bf16[32,3,320,128]{3,2,1,0:T(8,128)(2,1)} %bitcast.31, pred[32,3]{1,0:T(8,128)(4,1)S(1)} %reshape.339), kind=kLoop, calls=%fused_computation.3 | loop fusion | flops 3932160 | bytes 15728736 | tf_op jit(solution)/shard_map/jit(_where)/select_n | solution.py:31
  15.8 17.1 %all-to-all-start = ((bf16[32,3,320,128]{3,2,1,0:T(8,128)(2,1)}), bf16[32,3,320,128]{3,2,1,0:T(8,128)(2,1)}, u32[]{:S(2)}, u32[]{:S(2)}) async-start(bf16[32,3,320,128]{3,2,1,0:T(8,128)(2,1)} %broadcast_select_fusion), calls=%async_computation | async-start | bytes 15728640 | tf_op jit(solution)/shard_map/all_to_all | solution.py:32
  33.0 0.6 gather_fusion.2
  33.7 0.6 fusion.9
  39.9 332.2 %all-to-all-done = bf16[32,3,320,128]{3,2,1,0:T(8,128)(2,1)} async-done(((bf16[32,3,320,128]{3,2,1,0:T(8,128)(2,1)}), bf16[32,3,320,128]{3,2,1,0:T(8,128)(2,1)}, u32[]{:S(2)}, u32[]{:S(2)}) %all-to-all-start) | async-done | bytes 7864352 | tf_op jit(solution)/shard_map/all_to_all | solution.py:32
  372.1 1.0 constant_dynamic-slice_fusion.2
  373.1 0.1 copy.38
  373.2 0.1 copy.39
  373.3 0.1 copy.40
  373.5 3.1 collective-permute-start
  376.7 5.6 collective-permute-start.1
  382.3 4.8 collective-permute-done
  387.1 1.9 collective-permute-start.2
  389.1 6.7 %collective-permute-start.3 = (bf16[320,3,128]{0,2,1:T(8,128)(2,1)S(1)}, bf16[320,3,128]{0,2,1:T(8,128)(2,1)S(1)}, u32[]{:S(2)}, u32[]{:S(2)}) collective-permute-start(bf16[320,3,128]{0,2,1:T(8,128)(2,1)S(1)} %collective-permute-done.1), channel_id=1, source_target_pairs={{0,480},{32,0},{64,32},{96,64},{128,96},{160,128},{192,160},{224,1... | collective-permute-start | bytes 737288 | tf_op jit(solution)/shard_map/ppermute | solution.py:50
  395.7 3.9 collective-permute-done.2
  399.6 1.9 collective-permute-start.4
  401.5 6.7 %collective-permute-start.5 = (bf16[320,3,128]{0,2,1:T(8,128)(2,1)S(1)}, bf16[320,3,128]{0,2,1:T(8,128)(2,1)S(1)}, u32[]{:S(2)}, u32[]{:S(2)}) collective-permute-start(bf16[320,3,128]{0,2,1:T(8,128)(2,1)S(1)} %collective-permute-done.3), channel_id=1, source_target_pairs={{0,480},{32,0},{64,32},{96,64},{128,96},{160,128},{192,160},{224,1... | collective-permute-start | bytes 737288 | tf_op jit(solution)/shard_map/ppermute | solution.py:50
  408.2 3.0 collective-permute-done.4
  411.2 1.9 collective-permute-start.6
  413.1 6.7 %collective-permute-start.7 = (bf16[320,3,128]{0,2,1:T(8,128)(2,1)S(1)}, bf16[320,3,128]{0,2,1:T(8,128)(2,1)S(1)}, u32[]{:S(2)}, u32[]{:S(2)}) collective-permute-start(bf16[320,3,128]{0,2,1:T(8,128)(2,1)S(1)} %collective-permute-done.5), channel_id=1, source_target_pairs={{0,480},{32,0},{64,32},{96,64},{128,96},{160,128},{192,160},{224,1... | collective-permute-start | bytes 737288 | tf_op jit(solution)/shard_map/ppermute | solution.py:50
  419.8 2.2 collective-permute-done.6
  422.0 1.9 collective-permute-start.8
  423.9 6.7 %collective-permute-start.9 = (bf16[320,3,128]{0,2,1:T(8,128)(2,1)S(1)}, bf16[320,3,128]{0,2,1:T(8,128)(2,1)S(1)}, u32[]{:S(2)}, u32[]{:S(2)}) collective-permute-start(bf16[320,3,128]{0,2,1:T(8,128)(2,1)S(1)} %collective-permute-done.7), channel_id=1, source_target_pairs={{0,480},{32,0},{64,32},{96,64},{128,96},{160,128},{192,160},{224,1... | collective-permute-start | bytes 737288 | tf_op jit(solution)/shard_map/ppermute | solution.py:50
  430.6 2.2 collective-permute-done.8
  432.7 1.9 collective-permute-start.10
  434.7 6.7 %collective-permute-start.11 = (bf16[320,3,128]{0,2,1:T(8,128)(2,1)S(1)}, bf16[320,3,128]{0,2,1:T(8,128)(2,1)}, u32[]{:S(2)}, u32[]{:S(2)}) collective-permute-start(bf16[320,3,128]{0,2,1:T(8,128)(2,1)S(1)} %collective-permute-done.9), channel_id=1, source_target_pairs={{0,480},{32,0},{64,32},{96,64},{128,96},{160,128},{192,160},{224,1... | collective-permute-start | bytes 737288 | tf_op jit(solution)/shard_map/ppermute | solution.py:50
  441.4 2.2 collective-permute-done.10
  443.5 1.9 collective-permute-start.12
  445.5 6.8 %collective-permute-start.13 = (bf16[320,3,128]{0,2,1:T(8,128)(2,1)}, bf16[320,3,128]{0,2,1:T(8,128)(2,1)}, u32[]{:S(2)}, u32[]{:S(2)}) collective-permute-start(bf16[320,3,128]{0,2,1:T(8,128)(2,1)} %collective-permute-done.11), channel_id=1, source_target_pairs={{0,480},{32,0},{64,32},{96,64},{128,96},{160,128},{192,160},{224,1... | collective-permute-start | bytes 737288 | tf_op jit(solution)/shard_map/ppermute | solution.py:50
  452.2 2.2 collective-permute-done.12
  454.4 2.1 collective-permute-start.14
  456.8 0.2 reduce-window.8
  457.1 2.3 broadcast_in_dim.15
  459.4 3.5 dynamic_update_slice.48
  462.9 3.3 dynamic_update_slice.49
  466.2 4.0 dynamic_update_slice.50
  470.1 3.4 dynamic_update_slice.51
  473.5 3.5 dynamic_update_slice.52
  477.1 4.0 dynamic_update_slice.53
  481.0 4.0 dynamic_update_slice.54
  485.0 3.5 dynamic_update_slice.55
  488.5 3.5 dynamic_update_slice.56
  492.0 4.0 dynamic_update_slice.57
  496.0 4.0 dynamic_update_slice.58
  499.9 3.5 dynamic_update_slice.59
  503.4 3.6 dynamic_update_slice.60
  506.9 4.0 dynamic_update_slice.61
  510.9 4.0 dynamic_update_slice.62
  514.9 3.6 dynamic_update_slice.63
  518.5 5.5 fusion.1
  524.1 0.3 fusion.10
  524.4 0.1 fusion.3
  524.5 0.3 fusion.4
  524.8 42.4 %all_to_all.24 = f32[32,12,128]{2,1,0:T(8,128)S(1)} all-to-all(f32[32,12,128]{2,1,0:T(8,128)S(1)} %all_to_all.18), channel_id=1, replica_groups=mesh['grp'=16,'tp'=32] {'tp'}, dimensions={0} | all-to-all | bytes 393216 | tf_op jit(solution)/shard_map/all_to_all | solution.py:77
  567.3 0.9 copy.42
  (34 shorter events, 0.5 us)
Async XLA Ops:
  0.0 2.5 copy-start
  0.0 0.7 copy-start.1
  15.8 441.0 %copy-start.4 = (s32[1,4]{1,0:T(1,128)S(1)}, s32[1,4]{1,0:T(1,128)}, u32[]{:S(2)}) copy-start(s32[1,4]{1,0:T(1,128)} %param.7) | copy-start | bytes 52
  15.8 356.3 %all-to-all-start = ((bf16[32,3,320,128]{3,2,1,0:T(8,128)(2,1)}), bf16[32,3,320,128]{3,2,1,0:T(8,128)(2,1)}, u32[]{:S(2)}, u32[]{:S(2)}) async-start(bf16[32,3,320,128]{3,2,1,0:T(8,128)(2,1)} %broadcast_select_fusion), calls=%async_computation | async-start | bytes 15728640 | tf_op jit(solution)/shard_map/all_to_all | solution.py:32
  373.5 13.6 %collective-permute-start = (bf16[320,3,128]{0,2,1:T(8,128)(2,1)S(1)}, bf16[320,3,128]{0,2,1:T(8,128)(2,1)S(1)}, u32[]{:S(2)}, u32[]{:S(2)}) collective-permute-start(bf16[320,3,128]{0,2,1:T(8,128)(2,1)S(1)} %pad_maximum_fusion), channel_id=1, source_target_pairs={{0,32},{32,64},{64,96},{96,128},{128,160},{160,192},{192,224},{224... | collective-permute-start | bytes 737288 | tf_op jit(solution)/shard_map/ppermute | solution.py:45
  376.7 12.4 %collective-permute-start.1 = (bf16[320,3,128]{0,2,1:T(8,128)(2,1)S(1)}, bf16[320,3,128]{0,2,1:T(8,128)(2,1)S(1)}, u32[]{:S(2)}, u32[]{:S(2)}) collective-permute-start(bf16[320,3,128]{0,2,1:T(8,128)(2,1)S(1)} %pad_maximum_fusion), channel_id=1, source_target_pairs={{0,480},{32,0},{64,32},{96,64},{128,96},{160,128},{192,160},{224,1... | collective-permute-start | bytes 737288 | tf_op jit(solution)/shard_map/ppermute | solution.py:50
  387.1 12.5 %collective-permute-start.2 = (bf16[320,3,128]{0,2,1:T(8,128)(2,1)S(1)}, bf16[320,3,128]{0,2,1:T(8,128)(2,1)S(1)}, u32[]{:S(2)}, u32[]{:S(2)}) collective-permute-start(bf16[320,3,128]{0,2,1:T(8,128)(2,1)S(1)} %collective-permute-done), channel_id=1, source_target_pairs={{0,32},{32,64},{64,96},{96,128},{128,160},{160,192},{192,224},{224... | collective-permute-start | bytes 737288 | tf_op jit(solution)/shard_map/ppermute | solution.py:45
  389.1 12.5 %collective-permute-start.3 = (bf16[320,3,128]{0,2,1:T(8,128)(2,1)S(1)}, bf16[320,3,128]{0,2,1:T(8,128)(2,1)S(1)}, u32[]{:S(2)}, u32[]{:S(2)}) collective-permute-start(bf16[320,3,128]{0,2,1:T(8,128)(2,1)S(1)} %collective-permute-done.1), channel_id=1, source_target_pairs={{0,480},{32,0},{64,32},{96,64},{128,96},{160,128},{192,160},{224,1... | collective-permute-start | bytes 737288 | tf_op jit(solution)/shard_map/ppermute | solution.py:50
  399.6 11.6 %collective-permute-start.4 = (bf16[320,3,128]{0,2,1:T(8,128)(2,1)S(1)}, bf16[320,3,128]{0,2,1:T(8,128)(2,1)S(1)}, u32[]{:S(2)}, u32[]{:S(2)}) collective-permute-start(bf16[320,3,128]{0,2,1:T(8,128)(2,1)S(1)} %collective-permute-done.2), channel_id=1, source_target_pairs={{0,32},{32,64},{64,96},{96,128},{128,160},{160,192},{192,224},{224... | collective-permute-start | bytes 737288 | tf_op jit(solution)/shard_map/ppermute | solution.py:45
  401.5 11.6 %collective-permute-start.5 = (bf16[320,3,128]{0,2,1:T(8,128)(2,1)S(1)}, bf16[320,3,128]{0,2,1:T(8,128)(2,1)S(1)}, u32[]{:S(2)}, u32[]{:S(2)}) collective-permute-start(bf16[320,3,128]{0,2,1:T(8,128)(2,1)S(1)} %collective-permute-done.3), channel_id=1, source_target_pairs={{0,480},{32,0},{64,32},{96,64},{128,96},{160,128},{192,160},{224,1... | collective-permute-start | bytes 737288 | tf_op jit(solution)/shard_map/ppermute | solution.py:50
  411.2 10.8 %collective-permute-start.6 = (bf16[320,3,128]{0,2,1:T(8,128)(2,1)S(1)}, bf16[320,3,128]{0,2,1:T(8,128)(2,1)S(1)}, u32[]{:S(2)}, u32[]{:S(2)}) collective-permute-start(bf16[320,3,128]{0,2,1:T(8,128)(2,1)S(1)} %collective-permute-done.4), channel_id=1, source_target_pairs={{0,32},{32,64},{64,96},{96,128},{128,160},{160,192},{192,224},{224... | collective-permute-start | bytes 737288 | tf_op jit(solution)/shard_map/ppermute | solution.py:45
  413.1 10.8 %collective-permute-start.7 = (bf16[320,3,128]{0,2,1:T(8,128)(2,1)S(1)}, bf16[320,3,128]{0,2,1:T(8,128)(2,1)S(1)}, u32[]{:S(2)}, u32[]{:S(2)}) collective-permute-start(bf16[320,3,128]{0,2,1:T(8,128)(2,1)S(1)} %collective-permute-done.5), channel_id=1, source_target_pairs={{0,480},{32,0},{64,32},{96,64},{128,96},{160,128},{192,160},{224,1... | collective-permute-start | bytes 737288 | tf_op jit(solution)/shard_map/ppermute | solution.py:50
  422.0 10.8 %collective-permute-start.8 = (bf16[320,3,128]{0,2,1:T(8,128)(2,1)S(1)}, bf16[320,3,128]{0,2,1:T(8,128)(2,1)S(1)}, u32[]{:S(2)}, u32[]{:S(2)}) collective-permute-start(bf16[320,3,128]{0,2,1:T(8,128)(2,1)S(1)} %collective-permute-done.6), channel_id=1, source_target_pairs={{0,32},{32,64},{64,96},{96,128},{128,160},{160,192},{192,224},{224... | collective-permute-start | bytes 737288 | tf_op jit(solution)/shard_map/ppermute | solution.py:45
  423.9 10.8 %collective-permute-start.9 = (bf16[320,3,128]{0,2,1:T(8,128)(2,1)S(1)}, bf16[320,3,128]{0,2,1:T(8,128)(2,1)S(1)}, u32[]{:S(2)}, u32[]{:S(2)}) collective-permute-start(bf16[320,3,128]{0,2,1:T(8,128)(2,1)S(1)} %collective-permute-done.7), channel_id=1, source_target_pairs={{0,480},{32,0},{64,32},{96,64},{128,96},{160,128},{192,160},{224,1... | collective-permute-start | bytes 737288 | tf_op jit(solution)/shard_map/ppermute | solution.py:50
  432.7 10.8 %collective-permute-start.10 = (bf16[320,3,128]{0,2,1:T(8,128)(2,1)S(1)}, bf16[320,3,128]{0,2,1:T(8,128)(2,1)S(1)}, u32[]{:S(2)}, u32[]{:S(2)}) collective-permute-start(bf16[320,3,128]{0,2,1:T(8,128)(2,1)S(1)} %collective-permute-done.8), channel_id=1, source_target_pairs={{0,32},{32,64},{64,96},{96,128},{128,160},{160,192},{192,224},{224... | collective-permute-start | bytes 737288 | tf_op jit(solution)/shard_map/ppermute | solution.py:45
  434.7 10.8 %collective-permute-start.11 = (bf16[320,3,128]{0,2,1:T(8,128)(2,1)S(1)}, bf16[320,3,128]{0,2,1:T(8,128)(2,1)}, u32[]{:S(2)}, u32[]{:S(2)}) collective-permute-start(bf16[320,3,128]{0,2,1:T(8,128)(2,1)S(1)} %collective-permute-done.9), channel_id=1, source_target_pairs={{0,480},{32,0},{64,32},{96,64},{128,96},{160,128},{192,160},{224,1... | collective-permute-start | bytes 737288 | tf_op jit(solution)/shard_map/ppermute | solution.py:50
  443.5 1.9 copy-start.2
  443.5 10.9 %collective-permute-start.12 = (bf16[320,3,128]{0,2,1:T(8,128)(2,1)S(1)}, bf16[320,3,128]{0,2,1:T(8,128)(2,1)}, u32[]{:S(2)}, u32[]{:S(2)}) collective-permute-start(bf16[320,3,128]{0,2,1:T(8,128)(2,1)S(1)} %collective-permute-done.10), channel_id=1, source_target_pairs={{0,32},{32,64},{64,96},{96,128},{128,160},{160,192},{192,224},{224... | collective-permute-start | bytes 737288 | tf_op jit(solution)/shard_map/ppermute | solution.py:45
  445.5 65.4 %collective-permute-start.13 = (bf16[320,3,128]{0,2,1:T(8,128)(2,1)}, bf16[320,3,128]{0,2,1:T(8,128)(2,1)}, u32[]{:S(2)}, u32[]{:S(2)}) collective-permute-start(bf16[320,3,128]{0,2,1:T(8,128)(2,1)} %collective-permute-done.11), channel_id=1, source_target_pairs={{0,480},{32,0},{64,32},{96,64},{128,96},{160,128},{192,160},{224,1... | collective-permute-start | bytes 737288 | tf_op jit(solution)/shard_map/ppermute | solution.py:50
  454.4 60.5 %collective-permute-start.14 = (bf16[320,3,128]{0,2,1:T(8,128)(2,1)}, bf16[320,3,128]{0,2,1:T(8,128)(2,1)}, u32[]{:S(2)}, u32[]{:S(2)}) collective-permute-start(bf16[320,3,128]{0,2,1:T(8,128)(2,1)} %collective-permute-done.12), channel_id=1, source_target_pairs={{0,32},{32,64},{64,96},{96,128},{128,160},{160,192},{192,224},{224... | collective-permute-start | bytes 737288 | tf_op jit(solution)/shard_map/ppermute | solution.py:45
  462.9 37.1 %copy-start.3 = (bf16[320,3,128]{0,2,1:T(8,128)(2,1)S(1)}, bf16[320,3,128]{0,2,1:T(8,128)(2,1)}, u32[]{:S(2)}) copy-start(bf16[320,3,128]{0,2,1:T(8,128)(2,1)} %copy-done.2) | copy-start | bytes 737284
